TPU v7x, 128 devices: a whole 4x4x4 slice. The times are simulated.
128 devices in a mesh: gx: 16 (over z, y), gy: 8 (over x, core).
Axes of the slice: x: 4, y: 4, z: 4, core: 2. Of those that a mesh axis runs over, the one named last changes fastest.
Arguments:
- pumping: float32 [16, 4, 128, 1024], P(None, None, 'gx', 'gy'), may hold values from -1080 to 1080
- conductivity: float32 [4, 128, 1024], P(None, 'gx', 'gy'), may hold values from 0.2 to 5
- capacity: float32 [4, 128, 1024], P(None, 'gx', 'gy'), may hold values from 1 to 10
Outputs:
- solution: float32 [16, 4, 128, 1024], P(None, None, 'gx', 'gy')
- residual: float32 [16, 4, 128, 1024], P(None, None, 'gx', 'gy')
All inputs are finite; a program needn't handle non-finite values.
Results may differ from a plain program's by a relative error of at most 0.0035.
Values sent between devices are 32-bit elements; how exact they have to be, the bound alone decides.
A program may use at most 64 MiB of HBM per device.

v0:
```python
import jax
import jax.numpy as jnp
from jax import lax
from jax.sharding import PartitionSpec as P

RHS = 16
S = 4
CYCLES = 5
BASIS = 80


def padded_2(array, sides, width):
    for axis, dim in sides:
        devices, length = (lax.axis_size(axis), array.shape[dim])
        up = [(i, (i + 1) % devices) for i in range(devices - 1)]
        down = [(j, i) for i, j in up]
        last = lax.slice_in_dim(array, length - width, length, axis=dim)
        leading = lax.slice_in_dim(array, 0, width, axis=dim)
        before = lax.ppermute(last, axis, up)
        after = lax.ppermute(leading, axis, down)
        array = jnp.concatenate([before, array, after], axis=dim)
    return array


def face_terms(padded, storage):
    core = padded[1:-1, 1:-1, 1:-1]
    terms = (
        (core + padded[:-2, 1:-1, 1:-1]) * 0.5,
        (core + padded[2:, 1:-1, 1:-1]) * 0.5,
        (core + padded[1:-1, :-2, 1:-1]) * 0.5,
        (core + padded[1:-1, 2:, 1:-1]) * 0.5,
        (core + padded[1:-1, 1:-1, :-2]) * 0.5,
        (core + padded[1:-1, 1:-1, 2:]) * 0.5,
    )
    diagonal = storage + terms[0] + terms[1] + terms[2] + terms[3] + terms[4] + terms[5]
    return (terms, diagonal)


def apply_off(padded, terms):
    total = terms[0] * padded[:, :-2, 1:-1, 1:-1] + terms[1] * padded[:, 2:, 1:-1, 1:-1]
    total = total + terms[2] * padded[:, 1:-1, :-2, 1:-1] + terms[3] * padded[:, 1:-1, 2:, 1:-1]
    total = total + terms[4] * padded[:, 1:-1, 1:-1, :-2] + terms[5] * padded[:, 1:-1, 1:-1, 2:]
    return total


def small_solve(gram_all):
    shift_matrix = jnp.eye(BASIS, BASIS - RHS, dtype=jnp.float32) + jnp.eye(
        BASIS, BASIS - RHS, k=-RHS, dtype=jnp.float32
    )
    first_block = jnp.eye(BASIS, RHS, dtype=jnp.float32)
    hp = lax.Precision.HIGHEST
    gram_shift = jnp.dot(gram_all, shift_matrix, precision=hp)
    normal = jnp.dot(shift_matrix.T, gram_shift, precision=hp)
    right_side = jnp.dot(gram_shift.T, first_block, precision=hp)
    lower = jnp.linalg.cholesky(normal)
    y = jax.scipy.linalg.cho_solve((lower, True), right_side)
    coeffs = first_block - jnp.dot(shift_matrix, y, precision=hp)
    return (y, coeffs)


def shards(pumping, conductivity, capacity):
    hp = lax.Precision.HIGHEST
    shape = pumping.shape
    cond_halo = padded_2(conductivity, (("gx", 1), ("gy", 2)), 1)
    cond_pad = jnp.pad(cond_halo, ((1, 1), (0, 0), (0, 0)))
    terms, diagonal = face_terms(cond_pad, capacity)
    solution = jnp.zeros(shape, jnp.float32)
    residual = pumping / diagonal
    for restart in range(CYCLES):
        blocks = [residual]
        for k in range(S):
            bordered = padded_2(blocks[-1], (("gx", 2), ("gy", 3)), 1)
            padded = jnp.pad(bordered, ((0, 0), (1, 1), (0, 0), (0, 0)))
            blocks.append(-apply_off(padded, terms) / diagonal)
        stacked = jnp.concatenate(blocks, 0).reshape(BASIS, -1)
        local_gram = jnp.dot(stacked, stacked.T, precision=hp)
        gram_all = lax.psum(local_gram, ("gx", "gy"))
        y, coeffs = small_solve(gram_all)
        solution = solution + jnp.dot(y.T, stacked[: BASIS - RHS], precision=hp).reshape(shape)
        residual = jnp.dot(coeffs.T, stacked, precision=hp).reshape(shape)
    return (solution, residual)


def solution(mesh):
    return jax.shard_map(
        shards,
        mesh=mesh,
        in_specs=(P(None, None, "gx", "gy"), P(None, "gx", "gy"), P(None, "gx", "gy")),
        out_specs=(P(None, None, "gx", "gy"), P(None, None, "gx", "gy")),
        check_vma=False,
    )
```

profile of v0, /device:TPU:1, one launch (start us, length us, event | category | flops | bytes accessed | tf_op | source)
XLA Modules:
  0.0 885.2 jit_solution(18000092713170605420)
XLA Ops:
  10.6 5.1 collective-permute-start.2
  39.3 4.4 collective-permute-done.7
  44.5 4.6 collective-permute-start.8
  82.1 4.4 collective-permute-done.15
  103.1 4.4 collective-permute-done.19
  109.9 68.0 %psum.35 = f32[80,80]{1,0:T(8,128)S(1)} all-reduce(f32[80,80]{1,0:T(8,128)S(1)} %convolution_bitcast_fusion.4), channel_id=1, replica_groups=mesh['gx'=16,'gy'=8] {'gx','gy'}, use_global_device_ids=true, to_apply=%region_0.1 | all-reduce | flops 6400 | bytes 51200 | tf_op jit(solution)/shard_map/psum | solution.py:77
  179.8 5.8 cholesky.89
  187.0 4.9 custom-call.11
  201.0 4.9 collective-permute-start.22
  235.3 4.8 collective-permute-start.28
  280.8 66.5 %psum.36 = f32[80,80]{1,0:T(8,128)} all-reduce(f32[80,80]{1,0:T(8,128)} %convolution_bitcast_fusion.3), channel_id=1, replica_groups=mesh['gx'=16,'gy'=8] {'gx','gy'}, use_global_device_ids=true, to_apply=%region_3.6 | all-reduce | flops 6400 | bytes 51200 | tf_op jit(solution)/shard_map/psum | solution.py:77
  352.3 5.8 cholesky.100
  359.5 4.9 custom-call.12
  408.2 5.4 collective-permute-start.44
  425.6 4.4 collective-permute-done.47
  454.5 66.5 %psum.37 = f32[80,80]{1,0:T(8,128)S(1)} all-reduce(f32[80,80]{1,0:T(8,128)S(1)} %convolution_bitcast_fusion.2), channel_id=1, replica_groups=mesh['gx'=16,'gy'=8] {'gx','gy'}, use_global_device_ids=true, to_apply=%region_4.7 | all-reduce | flops 6400 | bytes 51200 | tf_op jit(solution)/shard_map/psum | solution.py:77
  525.3 5.8 cholesky.111
  532.4 4.9 custom-call.13
  547.1 4.8 collective-permute-start.54
  555.9 4.4 collective-permute-done.55
  575.9 4.4 collective-permute-done.59
  581.1 4.7 collective-permute-start.60
  626.7 66.7 %psum.38 = f32[80,80]{1,0:T(8,128)S(1)} all-reduce(f32[80,80]{1,0:T(8,128)S(1)} %convolution_bitcast_fusion.1), channel_id=1, replica_groups=mesh['gx'=16,'gy'=8] {'gx','gy'}, use_global_device_ids=true, to_apply=%region_5.8 | all-reduce | flops 6400 | bytes 51200 | tf_op jit(solution)/shard_map/psum | solution.py:77
  697.7 5.8 cholesky.122
  704.9 4.9 custom-call.14
  719.4 5.7 collective-permute-start.70
  729.1 4.4 collective-permute-done.71
  753.9 5.0 collective-permute-start.76
  776.2 4.5 collective-permute-start.80
  799.5 66.5 %psum.39 = f32[80,80]{1,0:T(8,128)S(1)} all-reduce(f32[80,80]{1,0:T(8,128)S(1)} %convolution_bitcast_fusion), channel_id=1, replica_groups=mesh['gx'=16,'gy'=8] {'gx','gy'}, use_global_device_ids=true, to_apply=%region_6.9 | all-reduce | flops 6400 | bytes 51200 | tf_op jit(solution)/shard_map/psum | solution.py:77
  867.9 5.8 cholesky.133
  875.1 4.9 custom-call.15
  (389 shorter events, 414.2 us)
Async XLA Ops:
  32.0 7.3 collective-permute-start.6
  35.3 8.4 collective-permute-start.7
  57.1 8.4 collective-permute-start.11
  78.1 8.4 collective-permute-start.15
  99.1 8.4 collective-permute-start.19
  201.0 8.9 %collective-permute-start.22 = (f32[16,4,10,1]{3,0,2,1:T(8,128)S(1)}, f32[16,4,10,1]{3,0,2,1:T(8,128)S(1)}, u32[]{:S(2)}, u32[]{:S(2)}) collective-permute-start(f32[16,4,10,1]{3,0,2,1:T(8,128)S(1)} %get-tuple-element.77), channel_id=1, source_target_pairs={{0,1},{1,2},{2,3},{3,4},{4,5},{5,6},{6,7},{8,9},{9,10},{10,11},{11... | collective-permute-start | bytes 7688 | tf_op jit(solution)/shard_map/ppermute | solution.py:19
  206.0 8.4 collective-permute-start.23
  222.8 7.3 collective-permute-start.26
  226.1 8.4 collective-permute-start.27
  245.2 7.2 collective-permute-start.30
  248.4 8.4 collective-permute-start.31
  266.2 7.2 collective-permute-start.34
  269.4 8.4 collective-permute-start.35
  374.5 8.4 collective-permute-start.38
  378.9 8.4 collective-permute-start.39
  399.0 8.4 collective-permute-start.43
  418.5 7.2 collective-permute-start.46
  421.6 8.4 collective-permute-start.47
  442.6 8.4 collective-permute-start.51
  547.1 8.8 collective-permute-start.54
  551.9 8.4 collective-permute-start.55
  571.9 8.4 collective-permute-start.59
  593.8 8.4 collective-permute-start.63
  611.9 7.4 collective-permute-start.66
  614.8 8.4 collective-permute-start.67
  719.4 9.7 %collective-permute-start.70 = (f32[16,4,10,1]{3,0,2,1:T(8,128)S(1)}, f32[16,4,10,1]{3,0,2,1:T(8,128)S(1)}, u32[]{:S(2)}, u32[]{:S(2)}) collective-permute-start(f32[16,4,10,1]{3,0,2,1:T(8,128)S(1)} %get-tuple-element.53), channel_id=1, source_target_pairs={{0,1},{1,2},{2,3},{3,4},{4,5},{5,6},{6,7},{8,9},{9,10},{10,11},{11... | collective-permute-start | bytes 7688 | tf_op jit(solution)/shard_map/ppermute | solution.py:19
  725.1 8.4 collective-permute-start.71
  741.5 7.2 collective-permute-start.74
  744.7 8.4 collective-permute-start.75
  753.9 7.6 collective-permute-start.76
  767.0 8.4 collective-permute-start.79
  788.7 8.4 collective-permute-start.83
  (64 other events, 720.1 us)
where the time goes:
time: 894 us; the launch traced here: 885 us
  blocking collectives  334 us (37%)
  starting transfers between devices  214 us (24%)
  waiting for transfers between devices  190 us (21%)
  other arithmetic  80.5 us (9%)
  matrix products  34 us (4%)
  local copies, waits for them, and re-layouts  30.1 us (3%)
    psum x5, blocking collectives, shards(): gram_all = lax.psum(local_gram, ('gx', 'gy'))  334 us
    ppermute x42, waiting for transfers between devices, padded_2(): after = lax.ppermute(leading, axis, down)  157 us
    ppermute x42, starting transfers between devices, padded_2(): before = lax.ppermute(last, axis, up)  145 us
    ppermute x42, starting transfers between devices, padded_2(): after = lax.ppermute(leading, axis, down)  68.6 us
    another operation x15, other arithmetic, small_solve(): lower = jnp.linalg.cholesky(normal)  32.6 us
    ppermute x42, waiting for transfers between devices, padded_2(): before = lax.ppermute(last, axis, up)  32.5 us
    another operation x10, other arithmetic, small_solve(): y = jax.scipy.linalg.cho_solve((lower, True), right_side)  27.7 us
    unnamed x46, local copies, waits for them, and re-layouts  18.2 us
  transfers between devices with their start and end apart: 84, of which 61 were waited for; matrix products, arithmetic and copies ran while one was open for 2% of the time, Pallas kernels for 0%

commit v1 on v0

--- a/solution.py
+++ b/solution.py
@@ -74,7 +74,7 @@
             blocks.append(-apply_off(padded, terms) / diagonal)
         stacked = jnp.concatenate(blocks, 0).reshape(BASIS, -1)
         local_gram = jnp.dot(stacked, stacked.T, precision=hp)
-        gram_all = lax.psum(local_gram, ("gx", "gy"))
+        gram_all = lax.psum(lax.psum(local_gram, "gy"), "gx")
         y, coeffs = small_solve(gram_all)
         solution = solution + jnp.dot(y.T, stacked[: BASIS - RHS], precision=hp).reshape(shape)
         residual = jnp.dot(coeffs.T, stacked, precision=hp).reshape(shape)

time: 894 us -> 1010 us (1.13)
  the two profiles are of different devices: /device:TPU:1 before, /device:TPU:0 now
where the time goes in v1:
time: 1010 us; the launch traced here: 998 us
  blocking collectives  507 us (50%)
  starting transfers between devices  207 us (20%)
  waiting for transfers between devices  137 us (14%)
  other arithmetic  80.6 us (8%)
  matrix products  34 us (3%)
  local copies, waits for them, and re-layouts  29.9 us (3%)
    psum x10, blocking collectives, shards(): gram_all = lax.psum(lax.psum(local_gram, 'gy'), 'gx')  507 us
    ppermute x42, starting transfers between devices, padded_2(): before = lax.ppermute(last, axis, up)  152 us
    ppermute x42, waiting for transfers between devices, padded_2(): after = lax.ppermute(leading, axis, down)  132 us
    ppermute x42, starting transfers between devices, padded_2(): after = lax.ppermute(leading, axis, down)  55.1 us
    another operation x15, other arithmetic, small_solve(): lower = jnp.linalg.cholesky(normal)  32.7 us
    another operation x10, other arithmetic, small_solve(): y = jax.scipy.linalg.cho_solve((lower, True), right_side)  27.8 us
  transfers between devices with their start and end apart: 84, of which 57 were waited for; matrix products, arithmetic and copies ran while one was open for 1% of the time, Pallas kernels for 0%

profile of v1, /device:TPU:0, one launch (start us, length us, event | category | flops | bytes accessed | tf_op | source)
XLA Modules:
  0.0 998.3 jit_solution(10252576720696878272)
XLA Ops:
  38.2 4.9 collective-permute-start.8
  49.1 6.1 collective-permute-start.10
  70.1 6.1 collective-permute-start.14
  91.1 6.1 collective-permute-start.18
  103.6 29.2 %psum.70 = f32[80,80]{1,0:T(8,128)S(1)} all-reduce(f32[80,80]{1,0:T(8,128)S(1)} %convolution_bitcast_fusion.4), channel_id=1, replica_groups=mesh['gx'=16,'gy'=8] {'gy'}, use_global_device_ids=true, to_apply=%region_0.1 | all-reduce | flops 6400 | bytes 51200 | tf_op jit(solution)/shard_map/psum | solution.py:77
  132.8 72.1 %psum.71 = f32[80,80]{1,0:T(8,128)S(1)} all-reduce(f32[80,80]{1,0:T(8,128)S(1)} %psum.70), channel_id=1, replica_groups=mesh['gx'=16,'gy'=8] {'gx'}, use_global_device_ids=true, to_apply=%region_1.2 | all-reduce | flops 6400 | bytes 51200 | tf_op jit(solution)/shard_map/psum | solution.py:77
  206.9 5.8 cholesky.89
  214.1 4.9 custom-call.11
  260.1 6.1 collective-permute-start.30
  281.1 6.1 collective-permute-start.34
  294.3 30.4 %psum.72 = f32[80,80]{1,0:T(8,128)} all-reduce(f32[80,80]{1,0:T(8,128)} %convolution_bitcast_fusion.3), channel_id=1, replica_groups=mesh['gx'=16,'gy'=8] {'gy'}, use_global_device_ids=true, to_apply=%region_4.7 | all-reduce | flops 6400 | bytes 51200 | tf_op jit(solution)/shard_map/psum | solution.py:77
  324.7 73.0 %psum.73 = f32[80,80]{1,0:T(8,128)} all-reduce(f32[80,80]{1,0:T(8,128)} %psum.72), channel_id=1, replica_groups=mesh['gx'=16,'gy'=8] {'gx'}, use_global_device_ids=true, to_apply=%region_5.8 | all-reduce | flops 6400 | bytes 51200 | tf_op jit(solution)/shard_map/psum | solution.py:77
  402.7 5.8 cholesky.100
  409.9 4.9 custom-call.12
  455.9 6.1 collective-permute-start.46
  477.1 5.9 collective-permute-start.50
  490.7 29.2 %psum.74 = f32[80,80]{1,0:T(8,128)S(1)} all-reduce(f32[80,80]{1,0:T(8,128)S(1)} %convolution_bitcast_fusion.2), channel_id=1, replica_groups=mesh['gx'=16,'gy'=8] {'gy'}, use_global_device_ids=true, to_apply=%region_6.9 | all-reduce | flops 6400 | bytes 51200 | tf_op jit(solution)/shard_map/psum | solution.py:77
  519.8 71.9 %psum.75 = f32[80,80]{1,0:T(8,128)S(1)} all-reduce(f32[80,80]{1,0:T(8,128)S(1)} %psum.74), channel_id=1, replica_groups=mesh['gx'=16,'gy'=8] {'gx'}, use_global_device_ids=true, to_apply=%region_7.10 | all-reduce | flops 6400 | bytes 51200 | tf_op jit(solution)/shard_map/psum | solution.py:77
  596.0 5.8 cholesky.111
  603.2 4.9 custom-call.13
  650.3 6.1 collective-permute-start.62
  671.3 6.1 collective-permute-start.66
  685.1 29.0 %psum.76 = f32[80,80]{1,0:T(8,128)S(1)} all-reduce(f32[80,80]{1,0:T(8,128)S(1)} %convolution_bitcast_fusion.1), channel_id=1, replica_groups=mesh['gx'=16,'gy'=8] {'gy'}, use_global_device_ids=true, to_apply=%region_8.11 | all-reduce | flops 6400 | bytes 51200 | tf_op jit(solution)/shard_map/psum | solution.py:77
  714.0 71.6 %psum.77 = f32[80,80]{1,0:T(8,128)S(1)} all-reduce(f32[80,80]{1,0:T(8,128)S(1)} %psum.76), channel_id=1, replica_groups=mesh['gx'=16,'gy'=8] {'gx'}, use_global_device_ids=true, to_apply=%region_9.12 | all-reduce | flops 6400 | bytes 51200 | tf_op jit(solution)/shard_map/psum | solution.py:77
  790.0 5.8 cholesky.122
  797.3 4.9 custom-call.14
  844.6 5.9 collective-permute-start.78
  865.8 6.1 collective-permute-start.82
  878.3 29.2 %psum.78 = f32[80,80]{1,0:T(8,128)S(1)} all-reduce(f32[80,80]{1,0:T(8,128)S(1)} %convolution_bitcast_fusion), channel_id=1, replica_groups=mesh['gx'=16,'gy'=8] {'gy'}, use_global_device_ids=true, to_apply=%region_10.13 | all-reduce | flops 6400 | bytes 51200 | tf_op jit(solution)/shard_map/psum | solution.py:77
  907.5 71.6 %psum.79 = f32[80,80]{1,0:T(8,128)S(1)} all-reduce(f32[80,80]{1,0:T(8,128)S(1)} %psum.78), channel_id=1, replica_groups=mesh['gx'=16,'gy'=8] {'gx'}, use_global_device_ids=true, to_apply=%region_11.14 | all-reduce | flops 6400 | bytes 51200 | tf_op jit(solution)/shard_map/psum | solution.py:77
  981.1 5.8 cholesky.133
  988.3 4.9 custom-call.15
  (394 shorter events, 362.7 us)
Async XLA Ops:
  23.9 5.8 collective-permute-start.5
  38.2 6.4 collective-permute-start.8
  43.1 5.8 collective-permute-start.9
  49.1 7.5 collective-permute-start.10
  64.1 5.8 collective-permute-start.13
  70.1 7.5 collective-permute-start.14
  85.1 5.8 collective-permute-start.17
  91.1 7.5 collective-permute-start.18
  222.8 5.8 collective-permute-start.21
  236.0 5.8 collective-permute-start.25
  242.0 5.9 collective-permute-start.26
  254.1 5.8 collective-permute-start.29
  260.1 7.5 collective-permute-start.30
  275.1 5.8 collective-permute-start.33
  281.1 7.5 collective-permute-start.34
  419.6 5.8 collective-permute-start.37
  432.8 5.8 collective-permute-start.41
  449.9 5.8 collective-permute-start.45
  455.9 7.4 collective-permute-start.46
  466.8 5.8 collective-permute-start.48
  471.1 5.8 collective-permute-start.49
  477.1 7.2 collective-permute-start.50
  632.2 5.9 collective-permute-start.58
  644.3 5.8 collective-permute-start.61
  650.3 7.5 collective-permute-start.62
  665.3 5.8 collective-permute-start.65
  671.3 10.4 %collective-permute-start.66 = (f32[16,4,10,1]{3,0,2,1:T(8,128)S(1)}, f32[16,4,10,1]{3,0,2,1:T(8,128)S(1)}, u32[]{:S(2)}, u32[]{:S(2)}) collective-permute-start(f32[16,4,10,1]{3,0,2,1:T(8,128)S(1)} %get-tuple-element.55), channel_id=1, source_target_pairs={{0,1},{1,2},{2,3},{3,4},{4,5},{5,6},{6,7},{8,9},{9,10},{10,11},{11... | collective-permute-start | bytes 7688 | tf_op jit(solution)/shard_map/ppermute | solution.py:19
  827.0 7.5 collective-permute-start.74
  844.6 8.7 collective-permute-start.78
  855.6 6.7 collective-permute-start.80
  859.8 5.8 collective-permute-start.81
  865.8 9.2 collective-permute-start.82
  (64 other events, 753.6 us)
